TPU v7x, 32 devices: a whole 2x2x4 slice. The times are simulated.
32 devices in a mesh: dp: 2 (over core), node: 4 (over y, x), pipe: 4 (over z).
Axes of the slice: x: 2, y: 2, z: 4, core: 2. Of those that a mesh axis runs over, the one named last changes fastest.
Arguments:
- final_hidden: bfloat16 [4096, 8192], P(('dp', 'node', 'pipe')), may hold values from -128 to 128
- value_head: bfloat16 [8192, 128], replicated, may hold values from -3 to 3
- norm_gain: bfloat16 [8192], replicated, may hold values from 0.5 to 1.5
- rewards: float32 [4096], P(('dp', 'node', 'pipe')), may hold values from -6 to 6
- old_values: float32 [4096], P(('dp', 'node', 'pipe')), may hold values from -6 to 6
- loss_mask: int32 [4096], P(('dp', 'node', 'pipe')), may hold values 0 or 1
- row_exp: int32 [32, 8192], P(('dp', 'node', 'pipe')), may hold values from -14 to -11
- gain_exp: int32 [32, 64], P(('dp', 'node', 'pipe')), may hold values from -16 to -7
- first_w: float32 [8192, 128], P(('dp', 'node', 'pipe')), may hold values from -4 to 4
- second_w: float32 [8192, 128], P(('dp', 'node', 'pipe')), may hold values from 0.01 to 1
- first_g: float32 [8192], P(('dp', 'node', 'pipe')), may hold values from -4 to 4
- second_g: float32 [8192], P(('dp', 'node', 'pipe')), may hold values from 0.01 to 1
Outputs:
- new_weight: bfloat16 [8192, 128], P(('dp', 'node'))
- new_gain: bfloat16 [8192], P(('dp', 'node'))
- first_w_new: float32 [8192, 128], P(('dp', 'node', 'pipe'))
- second_w_new: float32 [8192, 128], P(('dp', 'node', 'pipe'))
- first_g_new: float32 [8192], P(('dp', 'node', 'pipe'))
- second_g_new: float32 [8192], P(('dp', 'node', 'pipe'))
All inputs are finite; a program needn't handle non-finite values. No bound on the sum of `loss_mask` on one device may be relied on, other than what follows from the above.
Results may differ from a plain program's by a relative error of at most 0.0055.
Values may be sent and summed in bfloat16 or wider, within the bound.
A program may use at most 64 MiB of HBM per device.

v0:
```python
import functools
import math

import jax
import jax.numpy as jnp
from jax import lax
from jax.experimental import pallas as pl
from jax.experimental.pallas import tpu as pltpu
from jax.sharding import PartitionSpec as P

BINS = 128
GBLK = 128
SEQ = 32


LOGIT_SCALE = 0.0625
RETURN_LOW = -4.0
RETURN_HIGH = 4.0
TRACE_DECAY = 0.95
SAT_LIMIT = 448.0
LEARN_RATE = 0.02
FIRST_CORR = 0.19
SECOND_CORR = 0.0975
EPSILON = 1e-08
NORM_EPSILON = 1e-06


def gauss_targets(returns):
    width = (RETURN_HIGH - RETURN_LOW) / BINS
    spread = 0.75 * width
    bin_edges = RETURN_LOW + width * jnp.arange(BINS + 1).astype(jnp.float32)
    clamped = jnp.clip(returns, RETURN_LOW, RETURN_HIGH)
    cum_mass = 0.5 * (
        1.0
        + jax.scipy.special.erf((bin_edges[None, :] - clamped[:, None]) / (spread * math.sqrt(2.0)))
    )
    bin_mass = cum_mass[:, 1:] - cum_mass[:, :-1]
    return bin_mass / (cum_mass[:, -1:] - cum_mass[:, :1])


def gae_returns(rewards, old_values):
    reward_rows = rewards.reshape(-1, SEQ)
    value_rows = old_values.reshape(-1, SEQ)
    following = jnp.concatenate(
        [value_rows[:, 1:], jnp.zeros((value_rows.shape[0], 1), jnp.float32)], axis=1
    )
    td_error = reward_rows + following - value_rows
    row_pos = lax.broadcasted_iota(jnp.int32, (SEQ, SEQ), 0)
    col_pos = lax.broadcasted_iota(jnp.int32, (SEQ, SEQ), 1)
    offset = jnp.maximum(row_pos - col_pos, 0).astype(jnp.float32)
    kernel = jnp.where(row_pos >= col_pos, jnp.power(TRACE_DECAY, offset), 0.0)
    traced = jnp.dot(td_error, kernel, precision=lax.Precision.HIGHEST)
    return (traced + value_rows).reshape(-1)


def local_terms(hidden, gain, head, targets, mask, row_scale_exp, block_scale_exp):
    hidden_f = hidden.astype(jnp.float32)
    inv_rms = lax.rsqrt(jnp.mean(hidden_f * hidden_f, axis=1, keepdims=True) + NORM_EPSILON)
    normed = hidden_f * inv_rms
    scaled = (normed * gain.astype(jnp.float32)).astype(jnp.bfloat16)
    logits = LOGIT_SCALE * jnp.dot(scaled, head, preferred_element_type=jnp.float32)
    shifted = jnp.exp(logits - jnp.max(logits, axis=1, keepdims=True))
    probs_out = shifted / jnp.sum(shifted, axis=1, keepdims=True)
    errors = (LOGIT_SCALE * mask.astype(jnp.float32)[:, None] * (probs_out - targets)).astype(
        jnp.bfloat16
    )
    row_limit = SAT_LIMIT * jnp.exp2(row_scale_exp.astype(jnp.float32))
    block_limit = SAT_LIMIT * jnp.repeat(jnp.exp2(block_scale_exp.astype(jnp.float32)), GBLK)
    return inv_rms, errors, row_limit[None, :], block_limit[None, :]


def adam_update(param, grad, first, second):
    first_new = 0.9 * first + 0.1 * grad
    second_new = 0.95 * second + 0.05 * grad * grad
    update = first_new / FIRST_CORR / (jnp.sqrt(second_new / SECOND_CORR) + EPSILON)
    return (
        (param.astype(jnp.float32) - LEARN_RATE * update).astype(jnp.bfloat16),
        first_new,
        second_new,
    )


LANES = 128
GAIN_ROWS = 16
MESH = pl.DeviceIdType.MESH


def far_first(size):
    ring = [min(step, size - step) for step in range(size)]
    return sorted(range(size), key=lambda step: -ring[step])


def exchange(
    sizes,
    rows,
    hidden,
    inv_rms,
    errors_in,
    head,
    gain,
    row_limit,
    gain_limit,
    gain_blocks,
    first_w,
    second_w,
    first_g,
    second_g,
    new_weight,
    new_gain,
    first_w_new,
    second_w_new,
    first_g_new,
    second_g_new,
    quant,
    dp_buf,
    part,
    node_buf,
    pipe_out,
    pipe_buf,
    shared,
    dp_send,
    dp_recv,
    node_send,
    node_recv,
    pipe_send,
    pipe_recv,
    all_send,
    all_recv,
):
    n_dp, n_node, n_pipe = sizes
    me_dp = lax.axis_index("dp")
    me_node = lax.axis_index("node")
    me_pipe = lax.axis_index("pipe")
    gain_rows = first_g.shape[0]

    barrier = pltpu.get_barrier_semaphore()
    for axis, size, me in (("dp", n_dp, me_dp), ("node", n_node, me_node), ("pipe", n_pipe, me_pipe)):
        for step in range(1, size):
            pl.semaphore_signal(
                barrier, inc=1, device_id={axis: lax.rem(me + step, size)}, device_id_type=MESH
            )
    pl.semaphore_wait(barrier, n_dp + n_node + n_pipe - 3)

    order = far_first(n_pipe)

    def dp_copy(chunk, step):
        peer = lax.rem(me_dp + step, n_dp)
        return pltpu.make_async_remote_copy(
            src_ref=quant.at[peer, lax.rem(me_pipe + order[chunk], n_pipe)],
            dst_ref=dp_buf.at[step - 1, chunk],
            send_sem=dp_send.at[step - 1, chunk],
            recv_sem=dp_recv.at[step - 1, chunk],
            device_id={"dp": peer},
            device_id_type=MESH,
        )

    def node_copy(chunk, step):
        peer = lax.rem(me_node + step, n_node)
        return pltpu.make_async_remote_copy(
            src_ref=part.at[chunk, peer],
            dst_ref=node_buf.at[step - 1, chunk],
            send_sem=node_send.at[step - 1, chunk],
            recv_sem=node_recv.at[step - 1, chunk],
            device_id={"node": peer},
            device_id_type=MESH,
        )

    def pipe_copy(chunk):
        return pltpu.make_async_remote_copy(
            src_ref=pipe_out.at[chunk],
            dst_ref=pipe_buf.at[chunk],
            send_sem=pipe_send.at[chunk],
            recv_sem=pipe_recv.at[chunk],
            device_id={"pipe": lax.rem(me_pipe + order[chunk], n_pipe)},
            device_id_type=MESH,
        )

    def all_copy(step):
        return pltpu.make_async_remote_copy(
            src_ref=shared.at[me_pipe],
            dst_ref=shared.at[me_pipe],
            send_sem=all_send.at[step - 1],
            recv_sem=all_recv.at[step - 1],
            device_id={"pipe": lax.rem(me_pipe + step, n_pipe)},
            device_id_type=MESH,
        )

    tokens = hidden.shape[0]
    pad_rows = quant.shape[3] - rows
    errors = errors_in[...]
    errors_t = errors.astype(jnp.float32).T.astype(jnp.bfloat16)
    inverse = jnp.broadcast_to(inv_rms[...], (tokens, LANES))
    pad_index = lax.broadcasted_iota(jnp.int32, (pad_rows, LANES), 0)

    def multiply(dp, node, first_pipe, count):
        width = count * rows
        start = pl.multiple_of(((dp * n_node + node) * n_pipe + first_pipe) * rows, width)
        columns = pl.ds(start, width)
        normed = hidden[:, columns].astype(jnp.float32) * jnp.tile(inverse, (1, width // LANES))
        scaled = (normed * gain[:, columns]).astype(jnp.bfloat16)
        weight_t = jnp.dot(errors_t, scaled, preferred_element_type=jnp.float32)
        limit = row_limit[:, columns]
        weight = jnp.clip(weight_t, -limit, limit).T.astype(jnp.bfloat16)
        back_prop = lax.dot_general(
            errors, head[columns, :], (((1,), (1,)), ((), ())), preferred_element_type=jnp.float32
        )
        gain_part = jnp.sum(back_prop * normed, axis=0, keepdims=True)
        limit = gain_limit[:, columns]
        gain_part = jnp.clip(gain_part, -limit, limit)
        for index in range(count):
            pipe = first_pipe + index
            quant[dp, pipe, node, 0:rows] = weight[index * rows : (index + 1) * rows]
            padded = jnp.zeros((pad_rows, LANES), jnp.float32)
            for row in range(gain_rows):
                low = index * rows + row * LANES
                taken = min(LANES, rows - row * LANES)
                line = gain_part[:, low : low + taken]
                if taken < LANES:
                    line = jnp.concatenate([line, jnp.zeros((1, LANES - taken), jnp.float32)], axis=1)
                padded = jnp.where(pad_index == row, line, padded)
            quant[dp, pipe, node, rows : rows + pad_rows] = padded.astype(jnp.bfloat16)

    aligned = rows % LANES == 0

    def multiply_chunk(step, chunk):
        dp = lax.rem(me_dp + step, n_dp)
        if aligned:
            pipe = lax.rem(me_pipe + order[chunk], n_pipe)
            lax.fori_loop(0, n_node, lambda node, _: (multiply(dp, node, pipe, 1), _)[1], 0)
        elif chunk == 0:
            lax.fori_loop(0, n_node, lambda node, _: (multiply(dp, node, 0, n_pipe), _)[1], 0)

    for chunk in range(n_pipe):
        for step in range(1, n_dp):
            multiply_chunk(step, chunk)
            dp_copy(chunk, step).start()

    def dp_sum(chunk):
        own = lax.rem(me_pipe + order[chunk], n_pipe)
        multiply_chunk(0, chunk)
        for step in range(1, n_dp):
            dp_copy(chunk, step).wait_recv()
        for away in range(1, n_node + 1):
            node = lax.rem(me_node + away, n_node)
            total = quant[me_dp, own, node].astype(jnp.float32)
            for step in range(1, n_dp):
                total = total + dp_buf[step - 1, chunk, node].astype(jnp.float32)
            part[chunk, node] = total.astype(jnp.bfloat16)
            if away < n_node:
                node_copy(chunk, away).start()

    def node_sum(chunk):
        for step in range(1, n_node):
            node_copy(chunk, step).wait_recv()
        total = part[chunk, me_node].astype(jnp.float32)
        for step in range(1, n_node):
            total = total + node_buf[step - 1, chunk].astype(jnp.float32)
        pipe_out[chunk] = total.astype(jnp.bfloat16)
        if order[chunk] != 0:
            pipe_copy(chunk).start()

    for chunk in range(n_pipe):
        dp_sum(chunk)
        if chunk >= 1:
            node_sum(chunk - 1)
    node_sum(n_pipe - 1)

    for chunk in range(n_pipe - 1):
        pipe_copy(chunk).wait_recv()

    def adam(start, count, param, first, second, first_out, second_out):
        grad = pipe_out[n_pipe - 1, start : start + count].astype(jnp.float32)
        for chunk in range(n_pipe - 1):
            grad = grad + pipe_buf[chunk, start : start + count].astype(jnp.float32)
        new, first_new, second_new = adam_update(param, grad, first[...], second[...])
        first_out[...] = first_new
        second_out[...] = second_new
        return new

    position = (me_dp * n_node + me_node) * n_pipe + me_pipe
    own_weight = head[pl.ds(pl.multiple_of(position * rows, rows), rows), :]
    shared[me_pipe, rows : rows + gain_rows] = adam(
        rows, gain_rows, gain_blocks[position], first_g, second_g, first_g_new, second_g_new
    )
    shared[me_pipe, 0:rows] = adam(
        0, rows, own_weight, first_w, second_w, first_w_new, second_w_new
    )
    for step in range(1, n_pipe):
        all_copy(step).start()
    for chunk in range(n_pipe):
        for step in range(1, n_dp):
            dp_copy(chunk, step).wait_send()
        for step in range(1, n_node):
            node_copy(chunk, step).wait_send()
        if order[chunk] != 0:
            pipe_copy(chunk).wait_send()
    for step in range(1, n_pipe):
        all_copy(step).wait()
    for pipe in range(n_pipe):
        new_weight[pipe] = shared[pipe, 0:rows]
        new_gain[pipe] = shared[pipe, rows : rows + gain_rows]


def write_out(*refs):
    half = len(refs) // 2
    for source, target in zip(refs[:half], refs[half:]):
        target[...] = source[...]


def shards(
    final_hidden,
    value_head,
    norm_gain,
    rewards,
    old_values,
    loss_mask,
    row_exp,
    gain_exp,
    first_w,
    second_w,
    first_g,
    second_g,
):
    targets = gauss_targets(gae_returns(rewards, old_values))
    inv_rms, errors, row_limit, gain_limit = local_terms(
        final_hidden, norm_gain, value_head, targets, loss_mask, row_exp[0], gain_exp[0]
    )
    sizes = tuple(lax.axis_size(axis) for axis in ("dp", "node", "pipe"))
    n_dp, n_node, n_pipe = sizes
    rows = first_g.shape[0]
    bins = value_head.shape[1]
    gain_rows = -(-rows // bins)
    block_rows = rows + -(-gain_rows // GAIN_ROWS) * GAIN_ROWS

    def to_rows(values, total):
        lead = values.shape[:-1]
        values = jnp.pad(values, [(0, 0)] * len(lead) + [(0, total * bins - rows)])
        return values.reshape(lead + (total, bins))

    block = (block_rows, bins)
    vmem = pl.BlockSpec(memory_space=pltpu.VMEM)
    f32 = jnp.float32
    bf16 = jnp.bfloat16
    shapes = (
        jax.ShapeDtypeStruct((n_pipe, rows, bins), bf16),
        jax.ShapeDtypeStruct((n_pipe, gain_rows, bins), bf16),
        jax.ShapeDtypeStruct((rows, bins), f32),
        jax.ShapeDtypeStruct((rows, bins), f32),
        jax.ShapeDtypeStruct((gain_rows, bins), f32),
        jax.ShapeDtypeStruct((gain_rows, bins), f32),
    )
    buffers = [
        (n_dp, n_pipe, n_node) + block,
        (n_dp - 1, n_pipe, n_node) + block,
        (n_pipe, n_node) + block,
        (n_node - 1, n_pipe) + block,
        (n_pipe,) + block,
        (n_pipe,) + block,
        (n_pipe,) + block,
    ]
    held = 2 * sum(math.prod(shape) for shape in buffers)
    held += 2 * (final_hidden.size + value_head.size) + 24 * rows * bins
    updated = pl.pallas_call(
        functools.partial(exchange, sizes, rows),
        out_shape=shapes,
        in_specs=[vmem] * 12,
        out_specs=(vmem,) * 6,
        scratch_shapes=[pltpu.VMEM(shape, bf16) for shape in buffers]
        + [
            pltpu.SemaphoreType.DMA((n_dp - 1, n_pipe)),
            pltpu.SemaphoreType.DMA((n_dp - 1, n_pipe)),
            pltpu.SemaphoreType.DMA((n_node - 1, n_pipe)),
            pltpu.SemaphoreType.DMA((n_node - 1, n_pipe)),
            pltpu.SemaphoreType.DMA((n_pipe,)),
            pltpu.SemaphoreType.DMA((n_pipe,)),
            pltpu.SemaphoreType.DMA((n_pipe - 1,)),
            pltpu.SemaphoreType.DMA((n_pipe - 1,)),
        ],
        compiler_params=pltpu.CompilerParams(
            collective_id=0, has_side_effects=True, vmem_limit_bytes=held + (12 << 20)
        ),
    )(
        final_hidden,
        inv_rms,
        errors,
        value_head,
        norm_gain.astype(f32)[None, :],
        row_limit,
        gain_limit,
        to_rows(norm_gain.reshape(-1, rows), gain_rows),
        first_w,
        second_w,
        to_rows(first_g, gain_rows),
        to_rows(second_g, gain_rows),
    )
    new_weight, new_gain, first_w_new, second_w_new, first_g_new, second_g_new = pl.pallas_call(
        write_out,
        out_shape=shapes,
        in_specs=[vmem] * 6,
        out_specs=(vmem,) * 6,
        compiler_params=pltpu.CompilerParams(vmem_limit_bytes=8 << 20),
    )(*updated)

    def from_rows(values):
        lead = values.shape[:-2]
        return values.reshape(lead + (gain_rows * bins,))[..., :rows].reshape(-1)

    return (
        new_weight.reshape(n_pipe * rows, bins),
        from_rows(new_gain),
        first_w_new,
        second_w_new,
        from_rows(first_g_new),
        from_rows(second_g_new),
    )


def solution(mesh):
    return jax.shard_map(
        shards,
        mesh=mesh,
        in_specs=(
            P(("dp", "node", "pipe"), None),
            P(),
            P(),
            P(("dp", "node", "pipe")),
            P(("dp", "node", "pipe")),
            P(("dp", "node", "pipe")),
            P(("dp", "node", "pipe"), None),
            P(("dp", "node", "pipe"), None),
            P(("dp", "node", "pipe"), None),
            P(("dp", "node", "pipe"), None),
            P(("dp", "node", "pipe")),
            P(("dp", "node", "pipe")),
        ),
        out_specs=(
            P(("dp", "node"), None),
            P(("dp", "node")),
            P(("dp", "node", "pipe"), None),
            P(("dp", "node", "pipe"), None),
            P(("dp", "node", "pipe")),
            P(("dp", "node", "pipe")),
        ),
        check_vma=False,
    )
```

profile of v0, /device:TPU:0, one launch (start us, length us, event | category | flops | bytes accessed | tf_op | source)
XLA Modules:
  0.0 43.6 jit_solution(9628520755529667073)
XLA Ops:
  0.6 0.0 copy-start
  0.6 0.0 copy-start.4
  0.7 0.0 copy-start.7
  0.7 0.8 %convert_multiply_fusion.2 = f32[128]{0:T(128)S(1)} fusion(s32[128]{0:T(128)} %param.17), kind=kLoop, calls=%fused_computation.36 | loop fusion | flops 256 | bytes 1024 | tf_op jit(solution)/shard_map/mul | solution.py:64
  1.5 0.7 %multiply_bitcast_fusion = f32[64]{0:T(128)S(1)} fusion(s32[1,64]{1,0:T(1,128)} %param.19), kind=kLoop, calls=%fused_computation.35 | loop fusion | flops 192 | bytes 512 | tf_op jit(solution)/shard_map/mul | solution.py:68
  2.1 2.1 %fusion = f32[128]{0:T(128)S(1)} fusion(bf16[128,8192]{1,0:T(8,128)(2,1)} %hidden.1), kind=kLoop, calls=%fused_computation.2 | loop fusion | flops 3145600 | bytes 2097664 | tf_op jit(solution)/shard_map/reduce_sum | solution.py:58
  4.2 0.7 %reshape.99 = f32[4,32]{1,0:T(4,128)S(1)} reshape(f32[128]{0:T(128)} %param.16) | data formatting | bytes 1024 | tf_op jit(solution)/shard_map/reshape | solution.py:43
  5.0 0.1 slice.15
  5.0 0.7 %reshape.98 = f32[4,32]{1,0:T(4,128)S(1)} reshape(f32[128]{0:T(128)} %param.15) | data formatting | bytes 1024 | tf_op jit(solution)/shard_map/reshape | solution.py:42
  5.8 0.1 fusion.10
  5.9 0.1 min.12
  6.0 0.1 broadcast_in_dim.10
  6.1 0.0 copy-done.4
  6.1 0.0 copy-done.7
  6.1 0.1 exponential_multiply_fusion.row_limit
  6.2 0.1 copy.21.inv_rms
  6.3 0.0 copy-done
  6.3 0.0 copy-start.1
  6.3 0.0 copy-start.2
  6.3 0.0 copy-start.3
  6.3 0.0 copy-start.5
  6.4 0.0 copy-start.6
  6.4 2.6 %fusion.32 = (f32[128]{0:T(128)S(1)}, f32[128,128]{1,0:T(8,128)S(1)}) fusion(bf16[8192,128]{1,0:T(8,128)(2,1)} %head.1, bf16[128,8192]{1,0:T(8,128)(2,1)S(1)} %copy-done, f32[8192]{0:T(1024)S(1)} %convert_element_type.36, f32[128]{0:T(128)S(1)} %get-tuple-element.30), kind=kOutput, calls=%fused_computation.42 | convolution fusion | flops 272662400 | bytes 4293632 | tf_op jit(solution)/shard_map/dot_general | solution.py:61
  9.0 0.2 fusion.16
  9.2 0.1 add_multiply_fusion
  9.3 0.1 fusion.11
  9.4 0.2 fusion.15.errors_in
  9.6 0.0 copy-done.1
  9.6 0.0 copy-done.2
  9.6 0.0 copy-done.3
  9.6 0.0 copy-done.5
  9.6 0.0 copy-done.6
  9.6 33.2 %shard_map.163 = (bf16[4,256,128]{2,1,0:T(8,128)(2,1)S(1)}, bf16[4,2,128]{2,1,0:T(2,128)(2,1)S(1)}, f32[256,128]{1,0:T(8,128)S(1)}, f32[256,128]{1,0:T(8,128)S(1...) custom-call(bf16[128,8192]{1,0:T(8,128)(2,1)S(1)} %copy-done, f32[128,1]{1,0:T(8,128)S(1)} %copy.21.inv_rms, ...), custom_call_target="tpu_custom_call" | custom-call | tf_op jit(solution)/shard_map/pallas_call | solution.py:363
  42.8 0.8 %shard_map.164 = (bf16[4,256,128]{2,1,0:T(8,128)(2,1)}, bf16[4,2,128]{2,1,0:T(2,128)(2,1)}, f32[256,128]{1,0:T(8,128)}, f32[256,128]{1,0:T(8,128)}, f32[2,128]{1,0:T(2,128)}, /*index=5*/f32[2,128]{1,0:T(2,128)}) custom-call(bf16[4,256,128]{2,1,0:T(8,128)(2,1)S(1)} %get-tuple-element.18.refs_0_, bf16[4,2,128]{2,1,0:T(2,128)(2,1)S(1)} %get-tuple-element.19.refs_1_, ...), custom_call_target="tpu_custom_call" | custom-call | tf_op jit(solution)/shard_map/pallas_call | solution.py:396
  (3 shorter events, 0.0 us)
Async XLA Ops:
  0.6 5.7 %copy-start = (bf16[128,8192]{1,0:T(8,128)(2,1)S(1)}, bf16[128,8192]{1,0:T(8,128)(2,1)}, u32[]{:S(2)}) copy-start(bf16[128,8192]{1,0:T(8,128)(2,1)} %hidden.1) | copy-start | bytes 6291460
  0.6 5.4 %copy-start.4 = (bf16[8192]{0:T(1024)(128)(2,1)S(1)}, bf16[8192]{0:T(1024)(128)(2,1)}, u32[]{:S(2)}) copy-start(bf16[8192]{0:T(1024)(128)(2,1)} %param.14) | copy-start | bytes 49156
  0.7 5.5 %copy-start.7 = (s32[1,8192]{1,0:T(1,128)S(1)}, s32[1,8192]{1,0:T(1,128)}, u32[]{:S(2)}) copy-start(s32[1,8192]{1,0:T(1,128)} %param.18) | copy-start | bytes 98308
  6.3 3.3 %copy-start.1 = (bf16[8192,128]{1,0:T(8,128)(2,1)S(1)}, bf16[8192,128]{1,0:T(8,128)(2,1)}, u32[]{:S(2)}) copy-start(bf16[8192,128]{1,0:T(8,128)(2,1)} %head.1) | copy-start | bytes 6291460
  6.3 3.3 %copy-start.2 = (f32[256,128]{1,0:T(8,128)S(1)}, f32[256,128]{1,0:T(8,128)}, u32[]{:S(2)}) copy-start(f32[256,128]{1,0:T(8,128)} %first_w.1) | copy-start | bytes 393220
  6.3 3.3 %copy-start.3 = (f32[256,128]{1,0:T(8,128)S(1)}, f32[256,128]{1,0:T(8,128)}, u32[]{:S(2)}) copy-start(f32[256,128]{1,0:T(8,128)} %second_w.1) | copy-start | bytes 393220
  6.3 3.3 %copy-start.5 = (f32[256]{0:T(256)S(1)}, f32[256]{0:T(256)}, u32[]{:S(2)}) copy-start(f32[256]{0:T(256)} %param.22) | copy-start | bytes 3076
  6.4 3.3 %copy-start.6 = (f32[256]{0:T(256)S(1)}, f32[256]{0:T(256)}, u32[]{:S(2)}) copy-start(f32[256]{0:T(256)} %param.23) | copy-start | bytes 3076
where the time goes:
time: 43.8 us; the launch traced here: 43.6 us
  Pallas kernels  34 us (78%)
  other arithmetic  4.19 us (10%)
  matrix products  2.77 us (6%)
  local copies, waits for them, and re-layouts  1.87 us (4%)
  between operations  0.81 us (2%)
    pallas_call x1, Pallas kernels, shards(): pl.pallas_call(functools.partial(exchange, sizes, rows), out_shape=shapes...  33.2 us
    dot_general x1, matrix products, local_terms(): jnp.dot(scaled, head, preferred_element_type=jnp.float32)  2.63 us
    reduce_sum x1, other arithmetic, local_terms(): jnp.mean(hidden_f * hidden_f, axis=1, keepdims=True) + NORM_EPSILON  2.08 us

commit v1 on v0

--- a/solution.py
+++ b/solution.py
@@ -82,6 +82,7 @@
 
 LANES = 128
 GAIN_ROWS = 16
+VMEM_GRANT = 40000000
 MESH = pl.DeviceIdType.MESH
 
 
@@ -415,9 +416,579 @@
     )
 
 
+def ahead(n_pipe, me_pipe, step):
+    return lax.rem(me_pipe + step, n_pipe)
+
+
+def fused(
+    sizes,
+    rows,
+    hidden_in,
+    head_in,
+    gain_in,
+    rewards_in,
+    values_in,
+    mask_in,
+    row_exp_in,
+    gain_exp_in,
+    first_w_in,
+    second_w_in,
+    first_g_in,
+    second_g_in,
+    new_weight,
+    new_gain,
+    first_w_new,
+    second_w_new,
+    first_g_new,
+    second_g_new,
+    hidden,
+    head,
+    gain_raw,
+    rewards,
+    values,
+    mask,
+    row_exp,
+    gain_exp,
+    first_w,
+    second_w,
+    first_g,
+    second_g,
+    gain,
+    row_limit,
+    gain_limit,
+    quant,
+    dp_buf,
+    part,
+    near_buf,
+    far_out,
+    far_buf,
+    held,
+    pipe_out,
+    pipe_buf,
+    own,
+    gain_quant,
+    gain_dp,
+    gain_part,
+    gain_node,
+    gain_sum,
+    gain_pipe,
+    gain_all,
+    load_sem,
+    hidden_sem,
+    head_sem,
+    dp_send,
+    dp_recv,
+    near_send,
+    near_recv,
+    far_send,
+    far_recv,
+    pipe_send,
+    pipe_recv,
+    all_send,
+    all_recv,
+    gain_send,
+    gain_recv,
+):
+    n_dp, n_node, n_pipe = sizes
+    me_dp = lax.axis_index("dp")
+    me_node = lax.axis_index("node")
+    me_pipe = lax.axis_index("pipe")
+    me_high, me_low = me_node // 2, lax.rem(me_node, 2)
+    f32, bf16 = jnp.float32, jnp.bfloat16
+    halves = rows // LANES
+    tokens, width = hidden.shape
+    bins = head.shape[1]
+    chunks = hidden_sem.shape[0]
+    step_width = width // chunks
+    peer_dp = 1 - me_dp
+
+    small = (
+        (rewards_in, rewards),
+        (values_in, values),
+        (mask_in, mask),
+        (gain_in, gain_raw),
+        (row_exp_in, row_exp),
+        (gain_exp_in, gain_exp),
+        (first_w_in, first_w),
+        (second_w_in, second_w),
+        (first_g_in, first_g),
+        (second_g_in, second_g),
+    )
+    loads = [pltpu.make_async_copy(*pair, load_sem.at[index]) for index, pair in enumerate(small)]
+    hidden_loads = []
+    head_loads = []
+    for chunk in range(chunks):
+        span = pl.ds(chunk * step_width, step_width)
+        hidden_loads.append(
+            pltpu.make_async_copy(hidden_in.at[:, span], hidden.at[:, span], hidden_sem.at[chunk])
+        )
+        head_loads.append(
+            pltpu.make_async_copy(head_in.at[span, :], head.at[span, :], head_sem.at[chunk])
+        )
+    for copy in loads[:4]:
+        copy.start()
+    for chunk in range(chunks):
+        hidden_loads[chunk].start()
+        head_loads[chunk].start()
+    for copy in loads[4:]:
+        copy.start()
+
+    barrier = pltpu.get_barrier_semaphore()
+    for axis, size, me in (("dp", n_dp, me_dp), ("node", n_node, me_node), ("pipe", n_pipe, me_pipe)):
+        for step in range(1, size):
+            pl.semaphore_signal(
+                barrier, inc=1, device_id={axis: lax.rem(me + step, size)}, device_id_type=MESH
+            )
+
+    for copy in loads[:4]:
+        copy.wait()
+    at = lax.broadcasted_iota(jnp.int32, (tokens, tokens), 0)
+    later = lax.broadcasted_iota(jnp.int32, (tokens, tokens), 1)
+    reach = jnp.where(at // SEQ == later // SEQ, later - at, -1)
+    decay = jnp.exp(jnp.maximum(reach, 0).astype(f32) * math.log(TRACE_DECAY))
+    reward_part = jnp.where(reach >= 0, decay, 0.0) * rewards[...]
+    value_part = jnp.where(reach > 0, decay * ((1.0 - TRACE_DECAY) / TRACE_DECAY), 0.0) * values[...]
+    returns = jnp.sum(reward_part + value_part, axis=1, keepdims=True)
+    returns = jnp.clip(returns, RETURN_LOW, RETURN_HIGH)
+    counted = jnp.sum(
+        jnp.where(at == later, mask[...].astype(f32), 0.0), axis=1, keepdims=True
+    )
+    bin_width = (RETURN_HIGH - RETURN_LOW) / bins
+    sharp = 1.0 / (0.75 * bin_width * math.sqrt(2.0))
+    edge = lax.broadcasted_iota(jnp.int32, (tokens, bins), 1).astype(f32) * bin_width + RETURN_LOW
+    low_mass = lax.erf((edge - returns) * sharp)
+    high_mass = lax.erf((edge + bin_width - returns) * sharp)
+    targets = (high_mass - low_mass) / (high_mass[:, bins - 1 :] - low_mass[:, :1])
+    gain[...] = gain_raw[...].astype(f32)
+
+    groups = step_width // LANES
+    squares = jnp.zeros((tokens, LANES), f32)
+    logits = jnp.zeros((tokens, bins), f32)
+    for chunk in range(chunks):
+        hidden_loads[chunk].wait()
+        head_loads[chunk].wait()
+        pieces = []
+        for group in range(groups):
+            low = chunk * step_width + group * LANES
+            piece = hidden[:, low : low + LANES].astype(f32)
+            squares = squares + piece * piece
+            line = low // LANES
+            pieces.append((piece * gain[line : line + 1, :]).astype(bf16))
+        logits = logits + jnp.dot(
+            jnp.concatenate(pieces, axis=1),
+            head[chunk * step_width : (chunk + 1) * step_width, :],
+            preferred_element_type=f32,
+        )
+    for copy in loads[4:]:
+        copy.wait()
+    row_limit[...] = SAT_LIMIT * jnp.exp2(row_exp[...].astype(f32))
+    lines = gain.shape[0]
+    line_at = lax.broadcasted_iota(jnp.int32, (lines, lines), 0)
+    line_of = lax.broadcasted_iota(jnp.int32, (lines, lines), 1)
+    block_limit = SAT_LIMIT * jnp.exp2(gain_exp[...].astype(f32))
+    block_limit = jnp.sum(jnp.where(line_at == line_of, block_limit, 0.0), axis=1, keepdims=True)
+    gain_limit[...] = jnp.broadcast_to(block_limit, (lines, LANES))
+
+    mean_square = jnp.sum(squares, axis=1, keepdims=True) * (1.0 / width)
+    inv_rms = lax.rsqrt(mean_square + NORM_EPSILON)
+    logits = logits * (inv_rms * LOGIT_SCALE)
+    shifted = jnp.exp(logits - jnp.max(logits, axis=1, keepdims=True))
+    probs = shifted / jnp.sum(shifted, axis=1, keepdims=True)
+    scaled_errors = (counted * inv_rms * LOGIT_SCALE) * (probs - targets)
+    errors = scaled_errors.astype(bf16)
+    errors_t = scaled_errors.T.astype(bf16)
+
+    pl.semaphore_wait(barrier, n_dp + n_node + n_pipe - 3)
+
+    order = far_first(n_pipe)
+    phases = [(half, slot) for half in range(halves) for slot in range(n_pipe)]
+
+    def remote(source, target, send, recv, device_id):
+        return pltpu.make_async_remote_copy(
+            src_ref=source,
+            dst_ref=target,
+            send_sem=send,
+            recv_sem=recv,
+            device_id=device_id,
+            device_id_type=MESH,
+        )
+
+    def dp_copy(half, slot):
+        return remote(
+            quant.at[peer_dp, half, slot],
+            dp_buf.at[half, slot],
+            dp_send.at[half, slot],
+            dp_recv.at[half, slot],
+            {"dp": peer_dp},
+        )
+
+    def low_first(slot):
+        return slot % 2 == 0
+
+    def low_peer():
+        return me_high * 2 + 1 - me_low
+
+    def high_peer():
+        return (1 - me_high) * 2 + me_low
+
+    def near_copy(half, slot):
+        if low_first(slot):
+            source, peer = part.at[half, slot, :, 1 - me_low], low_peer()
+        else:
+            source, peer = part.at[half, slot, 1 - me_high], high_peer()
+        return remote(
+            source,
+            near_buf.at[half, slot],
+            near_send.at[half, slot],
+            near_recv.at[half, slot],
+            {"node": peer},
+        )
+
+    def far_copy(half, slot):
+        return remote(
+            far_out.at[half, slot],
+            far_buf.at[half, slot],
+            far_send.at[half, slot],
+            far_recv.at[half, slot],
+            {"node": high_peer() if low_first(slot) else low_peer()},
+        )
+
+    def pipe_copy(half, slot):
+        return remote(
+            pipe_out.at[half, slot],
+            pipe_buf.at[half, slot],
+            pipe_send.at[half, slot],
+            pipe_recv.at[half, slot],
+            {"pipe": ahead(n_pipe, me_pipe, order[slot])},
+        )
+
+    def all_copy(half, slot):
+        return remote(
+            new_weight.at[me_pipe, half],
+            new_weight.at[me_pipe, half],
+            all_send.at[half, slot],
+            all_recv.at[half, slot],
+            {"pipe": ahead(n_pipe, me_pipe, order[slot])},
+        )
+
+    def gain_copy(source, target, index, device_id):
+        return remote(source, target, gain_send.at[index], gain_recv.at[index], device_id)
+
+    gain_dp_copy = gain_copy(gain_quant.at[peer_dp], gain_dp, 0, {"dp": peer_dp})
+    gain_node_copies = []
+    for step in range(1, n_node):
+        peer = lax.rem(me_node + step, n_node)
+        gain_node_copies.append(
+            gain_copy(gain_part.at[peer], gain_node.at[step - 1], step, {"node": peer})
+        )
+    gain_pipe_copies = []
+    gain_all_copies = []
+    for step in range(1, n_pipe):
+        peer = ahead(n_pipe, me_pipe, step)
+        gain_pipe_copies.append(
+            gain_copy(
+                gain_sum.at[peer], gain_pipe.at[step - 1], n_node + step - 1, {"pipe": peer}
+            )
+        )
+        gain_all_copies.append(
+            gain_copy(
+                gain_all.at[me_pipe],
+                gain_all.at[me_pipe],
+                n_node + n_pipe + step - 2,
+                {"pipe": peer},
+            )
+        )
+
+    def multiply(dp, slot):
+        pipe = ahead(n_pipe, me_pipe, order[slot])
+        for node in range(n_node):
+            block = (dp * n_node + node) * n_pipe + pipe
+            span = pl.ds(pl.multiple_of(block * rows, rows), rows)
+            columns = hidden[:, span]
+            weight_t = jnp.dot(errors_t, columns, preferred_element_type=f32)
+            back_prop = lax.dot_general(
+                errors, head[span, :], (((1,), (1,)), ((), ())), preferred_element_type=f32
+            )
+            gain_line = jnp.sum(back_prop * columns.astype(f32), axis=0, keepdims=True)
+            for half in range(halves):
+                line = pl.ds(block * halves + half, 1)
+                low = half * LANES
+                limit = row_limit[line, :]
+                weight = weight_t[:, low : low + LANES] * gain[line, :]
+                quant[dp, half, slot, node // 2, node % 2] = jnp.clip(
+                    weight, -limit, limit
+                ).astype(bf16)
+                limit = gain_limit[line, :]
+                taken = jnp.clip(gain_line[:, low : low + LANES], -limit, limit)
+                gain_quant[dp, node, pipe, half] = taken.astype(bf16).astype(f32)
+
+    def add_dp(half, slot):
+        dp_copy(half, slot).wait_recv()
+        total = quant[me_dp, half, slot].astype(f32) + dp_buf[half, slot].astype(f32)
+        part[half, slot] = total.astype(bf16)
+        near_copy(half, slot).start()
+
+    def add_near(half, slot):
+        near_copy(half, slot).wait_recv()
+        if low_first(slot):
+            sent, kept = part[half, slot, 1 - me_high, me_low], part[half, slot, me_high, me_low]
+            other, mine = 1 - me_high, me_high
+        else:
+            sent, kept = part[half, slot, me_high, 1 - me_low], part[half, slot, me_high, me_low]
+            other, mine = 1 - me_low, me_low
+        total = sent.astype(f32) + near_buf[half, slot, other].astype(f32)
+        far_out[half, slot] = total.astype(bf16)
+        far_copy(half, slot).start()
+        held[half, slot] = kept.astype(f32) + near_buf[half, slot, mine].astype(f32)
+
+    def add_far(half, slot):
+        far_copy(half, slot).wait_recv()
+        total = held[half, slot] + far_buf[half, slot].astype(f32)
+        if order[slot] == 0:
+            own[half] = total
+        else:
+            pipe_out[half, slot] = total.astype(bf16)
+            pipe_copy(half, slot).start()
+
+    position = (me_dp * n_node + me_node) * n_pipe + me_pipe
+
+    def finish(half):
+        total = own[half]
+        for slot in range(n_pipe):
+            if order[slot] != 0:
+                pipe_copy(half, slot).wait_recv()
+                total = total + pipe_buf[half, slot].astype(f32)
+        low = half * LANES
+        start = pl.multiple_of(position * rows + low, LANES)
+        new, first, second = adam_update(
+            head[pl.ds(start, LANES), :],
+            total.T,
+            first_w[low : low + LANES, :],
+            second_w[low : low + LANES, :],
+        )
+        new_weight[me_pipe, half] = new
+        for slot in range(n_pipe):
+            if order[slot] != 0:
+                all_copy(half, slot).start()
+        first_w_new[low : low + LANES, :] = first
+        second_w_new[low : low + LANES, :] = second
+
+    def gain_add_dp():
+        gain_dp_copy.wait_recv()
+        gain_part[...] = gain_quant[me_dp] + gain_dp[...]
+        for copy in gain_node_copies:
+            copy.start()
+
+    def gain_add_node():
+        total = gain_part[me_node]
+        for index, copy in enumerate(gain_node_copies):
+            copy.wait_recv()
+            total = total + gain_node[index]
+        gain_sum[...] = total
+        for copy in gain_pipe_copies:
+            copy.start()
+
+    def gain_finish():
+        total = gain_sum[me_pipe]
+        for index, copy in enumerate(gain_pipe_copies):
+            copy.wait_recv()
+            total = total + gain_pipe[index]
+        for half in range(halves):
+            param = gain[pl.ds(position * halves + half, 1), :]
+            new, first, second = adam_update(param, total[half], first_g[half], second_g[half])
+            gain_all[me_pipe, half] = new.astype(f32)
+            first_g_new[half] = first
+            second_g_new[half] = second
+        for copy in gain_all_copies:
+            copy.start()
+
+    for slot in range(n_pipe):
+        multiply(peer_dp, slot)
+        for half in range(halves):
+            dp_copy(half, slot).start()
+    gain_dp_copy.start()
+    count = len(phases)
+
+    def advance(index):
+        if index < count:
+            add_dp(*phases[index])
+        if 0 <= index - 2 < count:
+            add_near(*phases[index - 2])
+        if 0 <= index - 3 < count:
+            add_far(*phases[index - 3])
+        for half in range(halves - 1):
+            if index - 3 == half * n_pipe + n_pipe + 1:
+                finish(half)
+
+    for slot in range(n_pipe):
+        multiply(me_dp, slot)
+        advance(slot)
+    gain_add_dp()
+    for index in range(n_pipe, count + 3):
+        advance(index)
+        if index == n_pipe:
+            gain_add_node()
+        if index == n_pipe + 2:
+            gain_finish()
+    finish(halves - 1)
+
+    for half, slot in phases:
+        dp_copy(half, slot).wait_send()
+        near_copy(half, slot).wait_send()
+        far_copy(half, slot).wait_send()
+        if order[slot] != 0:
+            pipe_copy(half, slot).wait_send()
+    gain_dp_copy.wait_send()
+    for copy in gain_node_copies + gain_pipe_copies:
+        copy.wait_send()
+    for copy in gain_all_copies:
+        copy.wait()
+    new_gain[...] = gain_all[...].reshape(n_pipe * halves, LANES).astype(bf16)
+    for half, slot in phases:
+        if order[slot] != 0:
+            all_copy(half, slot).wait()
+
+
+def send_home(*refs):
+    count = (len(refs) - 1) // 2
+    sems = refs[-1]
+    copies = [
+        pltpu.make_async_copy(refs[index], refs[count + index], sems.at[index])
+        for index in range(count)
+    ]
+    for copy in copies:
+        copy.start()
+    for copy in copies:
+        copy.wait()
+
+
+def fused_shards(
+    final_hidden,
+    value_head,
+    norm_gain,
+    rewards,
+    old_values,
+    loss_mask,
+    row_exp,
+    gain_exp,
+    first_w,
+    second_w,
+    first_g,
+    second_g,
+):
+    sizes = tuple(lax.axis_size(axis) for axis in ("dp", "node", "pipe"))
+    n_dp, n_node, n_pipe = sizes
+    rows = first_g.shape[0]
+    tokens, width = final_hidden.shape
+    bins = value_head.shape[1]
+    halves = rows // LANES
+    lines = width // LANES
+    chunks = max(1, width // 1024)
+    f32, bf16, i32 = jnp.float32, jnp.bfloat16, jnp.int32
+    vmem = pl.BlockSpec(memory_space=pltpu.VMEM)
+    hbm = pl.BlockSpec(memory_space=pltpu.HBM)
+    tile = (bins, LANES)
+    shapes = (
+        jax.ShapeDtypeStruct((n_pipe, halves, LANES, bins), bf16),
+        jax.ShapeDtypeStruct((n_pipe * halves, LANES), bf16),
+        jax.ShapeDtypeStruct((rows, bins), f32),
+        jax.ShapeDtypeStruct((rows, bins), f32),
+        jax.ShapeDtypeStruct((halves, 1, LANES), f32),
+        jax.ShapeDtypeStruct((halves, 1, LANES), f32),
+    )
+    buffers = [
+        ((tokens, width), bf16),
+        ((width, bins), bf16),
+        ((lines, LANES), bf16),
+        ((1, tokens), f32),
+        ((1, tokens), f32),
+        ((1, tokens), i32),
+        ((lines, LANES), i32),
+        ((1, lines), i32),
+        ((rows, bins), f32),
+        ((rows, bins), f32),
+        ((halves, 1, LANES), f32),
+        ((halves, 1, LANES), f32),
+        ((lines, LANES), f32),
+        ((lines, LANES), f32),
+        ((lines, LANES), f32),
+        ((n_dp, halves, n_pipe, 2, 2) + tile, bf16),
+        ((halves, n_pipe, 2, 2) + tile, bf16),
+        ((halves, n_pipe, 2, 2) + tile, bf16),
+        ((halves, n_pipe, 2) + tile, bf16),
+        ((halves, n_pipe) + tile, bf16),
+        ((halves, n_pipe) + tile, bf16),
+        ((halves, n_pipe) + tile, f32),
+        ((halves, n_pipe) + tile, bf16),
+        ((halves, n_pipe) + tile, bf16),
+        ((halves,) + tile, f32),
+        ((n_dp, n_node, n_pipe, halves, 1, LANES), f32),
+        ((n_node, n_pipe, halves, 1, LANES), f32),
+        ((n_node, n_pipe, halves, 1, LANES), f32),
+        ((n_node - 1, n_pipe, halves, 1, LANES), f32),
+        ((n_pipe, halves, 1, LANES), f32),
+        ((n_pipe - 1, halves, 1, LANES), f32),
+        ((n_pipe, halves, 1, LANES), f32),
+    ]
+    dma = pltpu.SemaphoreType.DMA
+    semaphores = [(10,), (chunks,), (chunks,)]
+    semaphores += [(halves, n_pipe)] * 10
+    semaphores += [(n_node + 2 * n_pipe - 2,)] * 2
+    updated = pl.pallas_call(
+        functools.partial(fused, sizes, rows),
+        out_shape=shapes,
+        in_specs=[hbm] * 12,
+        out_specs=(vmem,) * 6,
+        scratch_shapes=[pltpu.VMEM(shape, kind) for shape, kind in buffers]
+        + [dma(shape) for shape in semaphores],
+        compiler_params=pltpu.CompilerParams(
+            collective_id=0, has_side_effects=True, vmem_limit_bytes=VMEM_GRANT
+        ),
+    )(
+        *[pltpu.with_memory_space_constraint(value, pltpu.HBM) for value in (
+        final_hidden,
+        value_head,
+        norm_gain.reshape(lines, LANES),
+        rewards.reshape(1, tokens),
+        old_values.reshape(1, tokens),
+        loss_mask.reshape(1, tokens),
+        row_exp.reshape(lines, LANES),
+        gain_exp,
+        first_w,
+        second_w,
+        first_g.reshape(halves, 1, LANES),
+        second_g.reshape(halves, 1, LANES),
+        )]
+    )
+    new_weight, new_gain, first_w_new, second_w_new, first_g_new, second_g_new = pl.pallas_call(
+        send_home,
+        out_shape=shapes,
+        in_specs=[vmem] * 6,
+        out_specs=(hbm,) * 6,
+        scratch_shapes=[dma((6,))],
+        compiler_params=pltpu.CompilerParams(vmem_limit_bytes=8 << 20),
+    )(*updated)
+    return (
+        new_weight.reshape(n_pipe * rows, bins),
+        new_gain.reshape(-1),
+        first_w_new,
+        second_w_new,
+        first_g_new.reshape(-1),
+        second_g_new.reshape(-1),
+    )
+
+
+def any_shards(*args):
+    hidden, head, first_g = args[0], args[1], args[10]
+    fits = lax.axis_size("dp") == 2 and lax.axis_size("node") == 4 and lax.axis_size("pipe") > 1
+    fits = fits and first_g.shape[0] % LANES == 0 and head.shape[1] == LANES
+    fits = fits and hidden.shape[0] % LANES == 0 and hidden.shape[1] % 1024 == 0
+    return fused_shards(*args) if fits else shards(*args)
+
+
 def solution(mesh):
     return jax.shard_map(
-        shards,
+        any_shards,
         mesh=mesh,
         in_specs=(
             P(("dp", "node", "pipe"), None),

time: 43.8 us -> 38 us (0.87)
  other arithmetic: 4.19 us -> 0 us
  Pallas kernels: 34 us -> 37.2 us
  matrix products: 2.77 us -> 0 us
  local copies, waits for them, and re-layouts: 1.87 us -> 0 us
    pallas_call x2, Pallas kernels: 34 us -> 37.2 us  [the longest x1 36.4 us: fused_shards(): pl.pallas_call(functools.partial(fused, sizes, rows), out_shape=shapes, i...]
    dot_general x2 -> x0, matrix products: 2.77 us -> none  [the longest x1 2.63 us: local_terms(): jnp.dot(scaled, head, preferred_element_type=jnp.float32)]
    reduce_sum x2 -> x0, other arithmetic: 2.27 us -> none  [the longest x1 2.08 us: local_terms(): jnp.mean(hidden_f * hidden_f, axis=1, keepdims=True) + NORM_EPSILON]
    mul x4 -> x0, other arithmetic: 1.63 us -> none  [the longest x1 0.8 us: local_terms(): LOGIT_SCALE * mask.astype(jnp.float32)[:, None] * (probs_out - targets)]
    reshape x2 -> x0, local copies, waits for them, and re-layouts: 1.48 us -> none  [the longest x1 0.74 us: gae_returns(): value_rows = old_values.reshape(-1, SEQ)]
where the time goes in v1:
time: 38 us; the launch traced here: 37.9 us
  Pallas kernels  37.2 us (98%)
  between operations  0.64 us (2%)
    pallas_call x1, Pallas kernels, fused_shards(): pl.pallas_call(functools.partial(fused, sizes, rows), out_shape=shapes, i...  36.4 us
    pallas_call x1, Pallas kernels, fused_shards(): pl.pallas_call(send_home, out_shape=shapes, in_specs=[vmem] * 6, out_spec...  0.85 us

profile of v1, /device:TPU:0, one launch (start us, length us, event | category | flops | bytes accessed | tf_op | source)
XLA Modules:
  0.0 37.9 jit_solution(9716025468935436229)
XLA Ops:
  0.6 36.4 %shard_map.163 = (bf16[4,2,128,128]{3,2,1,0:T(8,128)(2,1)S(1)}, bf16[8,128]{1,0:T(8,128)(2,1)S(1)}, f32[256,128]{1,0:T(8,128)S(1)}, f32[256,128]{1,0:T(8,128)S(1...) custom-call(bf16[128,8192]{1,0:T(8,128)(2,1)} %hidden_in.1, bf16[8192,128]{1,0:T(8,128)(2,1)} %head_in.1, ...), custom_call_target="tpu_custom_call" | custom-call | tf_op jit(solution)/shard_map/pallas_call | solution.py:937
  37.0 0.8 %shard_map.164 = (bf16[4,2,128,128]{3,2,1,0:T(8,128)(2,1)}, bf16[8,128]{1,0:T(8,128)(2,1)}, f32[256,128]{1,0:T(8,128)}, f32[256,128]{1,0:T(8,128)}, f32[2,1,128]{2,1,0:T(1,128)}, /*index=5*/f32[2,1,128]{2,1,0:T(1,128)}) custom-call(bf16[4,2,128,128]{3,2,1,0:T(8,128)(2,1)S(1)} %get-tuple-element.18.refs_0_, bf16[8,128]{1,0:T(8,128)(2,1)S(1)} %get-tuple-element.19.refs_1_, ...), custom_call_target="tpu_custom_call" | custom-call | tf_op jit(solution)/shard_map/pallas_call | solution.py:963

commit v2 on v1

--- a/solution.py
+++ b/solution.py
@@ -83,6 +83,9 @@
 LANES = 128
 GAIN_ROWS = 16
 VMEM_GRANT = 40000000
+NEAR_LAG = 4
+FAR_LAG = 4
+DONE_LAG = 4
 MESH = pl.DeviceIdType.MESH
 
 
@@ -808,28 +811,30 @@
             dp_copy(half, slot).start()
     gain_dp_copy.start()
     count = len(phases)
+    near_lag = min(NEAR_LAG, count)
+    far_lag = near_lag + min(FAR_LAG, count)
 
     def advance(index):
         if index < count:
             add_dp(*phases[index])
-        if 0 <= index - 2 < count:
-            add_near(*phases[index - 2])
-        if 0 <= index - 3 < count:
-            add_far(*phases[index - 3])
+        if 0 <= index - near_lag < count:
+            add_near(*phases[index - near_lag])
+            if index - near_lag == n_pipe:
+                gain_add_node()
+        if 0 <= index - far_lag < count:
+            add_far(*phases[index - far_lag])
+            if index - far_lag == n_pipe:
+                gain_finish()
         for half in range(halves - 1):
-            if index - 3 == half * n_pipe + n_pipe + 1:
+            if index - far_lag == min(half * n_pipe + n_pipe - 1 + DONE_LAG, count - 1):
                 finish(half)
 
     for slot in range(n_pipe):
         multiply(me_dp, slot)
         advance(slot)
     gain_add_dp()
-    for index in range(n_pipe, count + 3):
+    for index in range(n_pipe, count + far_lag):
         advance(index)
-        if index == n_pipe:
-            gain_add_node()
-        if index == n_pipe + 2:
-            gain_finish()
     finish(halves - 1)
 
     for half, slot in phases:
@@ -980,7 +985,7 @@
 
 def any_shards(*args):
     hidden, head, first_g = args[0], args[1], args[10]
-    fits = lax.axis_size("dp") == 2 and lax.axis_size("node") == 4 and lax.axis_size("pipe") > 1
+    fits = lax.axis_size("dp") == 2 and lax.axis_size("node") == 4 and lax.axis_size("pipe") == 4
     fits = fits and first_g.shape[0] % LANES == 0 and head.shape[1] == LANES
     fits = fits and hidden.shape[0] % LANES == 0 and hidden.shape[1] % 1024 == 0
     return fused_shards(*args) if fits else shards(*args)

time: 38 us -> 31.8 us (0.84)
  Pallas kernels: 37.2 us -> 31 us
    pallas_call x1, Pallas kernels: 36.4 us -> 30.1 us  [fused_shards(): pl.pallas_call(functools.partial(fused, sizes, rows), out_shape=shapes, i...]
where the time goes in v2:
time: 31.8 us; the launch traced here: 31.6 us
  Pallas kernels  31 us (97%)
  between operations  0.64 us (2%)
    pallas_call x1, Pallas kernels, fused_shards(): pl.pallas_call(functools.partial(fused, sizes, rows), out_shape=shapes, i...  30.1 us
    pallas_call x1, Pallas kernels, fused_shards(): pl.pallas_call(send_home, out_shape=shapes, in_specs=[vmem] * 6, out_spec...  0.85 us

profile of v2, /device:TPU:0, one launch (start us, length us, event | category | flops | bytes accessed | tf_op | source)
XLA Modules:
  0.0 31.6 jit_solution(5972565275747064753)
XLA Ops:
  0.6 30.1 %shard_map.163 = (bf16[4,2,128,128]{3,2,1,0:T(8,128)(2,1)S(1)}, bf16[8,128]{1,0:T(8,128)(2,1)S(1)}, f32[256,128]{1,0:T(8,128)S(1)}, f32[256,128]{1,0:T(8,128)S(1...) custom-call(bf16[128,8192]{1,0:T(8,128)(2,1)} %hidden_in.1, bf16[8192,128]{1,0:T(8,128)(2,1)} %head_in.1, ...), custom_call_target="tpu_custom_call" | custom-call | tf_op jit(solution)/shard_map/pallas_call | solution.py:942
  30.8 0.8 %shard_map.164 = (bf16[4,2,128,128]{3,2,1,0:T(8,128)(2,1)}, bf16[8,128]{1,0:T(8,128)(2,1)}, f32[256,128]{1,0:T(8,128)}, f32[256,128]{1,0:T(8,128)}, f32[2,1,128]{2,1,0:T(1,128)}, /*index=5*/f32[2,1,128]{2,1,0:T(1,128)}) custom-call(bf16[4,2,128,128]{3,2,1,0:T(8,128)(2,1)S(1)} %get-tuple-element.18.refs_0_, bf16[8,128]{1,0:T(8,128)(2,1)S(1)} %get-tuple-element.19.refs_1_, ...), custom_call_target="tpu_custom_call" | custom-call | tf_op jit(solution)/shard_map/pallas_call | solution.py:968
